TPU v7x, 256 devices: a whole 4x4x8 slice. The times are simulated.
256 devices in a mesh: rows: 8 (over z), cols: 32 (over y, x, core).
Axes of the slice: x: 4, y: 4, z: 8, core: 2. Of those that a mesh axis runs over, the one named last changes fastest.
Arguments:
- whitened: float32 [3, 1048576], P(None, ('rows', 'cols')), may hold values from -6 to 6
- cotangent: bfloat16 [64, 1048576], P(None, ('rows', 'cols')), may hold values from -6 to 6
- lift_weight: float32 [64, 3], replicated, may hold values from -3.5 to 3.5
- conv_now: bfloat16 [3, 128, 64], replicated, may hold values from -0.5 to 0.5
- conv_past: bfloat16 [3, 128, 64], replicated, may hold values from -0.5 to 0.5
- mix_weight: bfloat16 [3, 64, 64], replicated, may hold values from -0.75 to 0.75
- dilations: int32 [3], replicated, may hold values from 64 to 256, as said below
- psd_bin: int32 [4096, 32, 8], P(None, 'cols', 'rows'), may hold values from 0 to 1023, as said below
- psd_weight: float32 [2, 1024], replicated, may hold values from 0.2 to 5
Outputs:
- data_grad: float32 [3, 1048576], P(None, ('rows', 'cols'))
- grad_now: float32 [3, 128, 64], replicated
- grad_past: float32 [3, 128, 64], replicated
- grad_mix: float32 [3, 64, 64], replicated
- grad_lift: float32 [64, 3], replicated
Inputs may be any that keep to these rules, and one draw needn't show every extreme that they name: `dilations`: multiples of 4; one layer has 64, one has 256. `psd_bin`: frequencies k and 1048576 - k have the same bin.
All inputs are finite; a program needn't handle non-finite values.
Results may differ from a plain program's by a relative error of at most 0.0068.
Values may be sent and summed in bfloat16 or wider, within the bound.
No kernel may reach another device: no remote copies, remote signals or barrier semaphores. Data moves between devices by JAX's collectives and lax.ppermute only.
A program may use at most 64 MiB of HBM per device.

v0:
```python
import math
import jax
import jax.numpy as jnp
from jax import lax
from jax.sharding import PartitionSpec as P

DMAX = 256


def from_behind(array, axis, by):
    peers = lax.axis_size(axis)
    pairs = [(i, i + by) for i in range(peers) if 0 <= i + by < peers]
    return lax.ppermute(array, axis, pairs)


def lifted(lift_weight, inputs):
    return (
        lift_weight[:, 0:1] * inputs[0:1]
        + lift_weight[:, 1:2] * inputs[1:2]
        + lift_weight[:, 2:3] * inputs[2:3]
    )


def delayed(field_b, delay, before):
    joined = jnp.concatenate([before, field_b], axis=1)
    start_at = before.shape[1] - delay
    return lax.dynamic_slice_in_dim(joined, start_at, field_b.shape[1], 1)


def advanced(values, delay, head_rim):
    joined = jnp.concatenate([values, head_rim], axis=1)
    return lax.dynamic_slice_in_dim(joined, delay, values.shape[1], 1)


def gated_layer(field_now, field_b, before, weight_now, weight_past, weight_mix, delay):
    channel_count = weight_mix.shape[0]
    past_b = delayed(field_b, delay, before)
    pre_act = jnp.dot(weight_now, field_b, preferred_element_type=jnp.float32) + jnp.dot(
        weight_past, past_b, preferred_element_type=jnp.float32
    )
    tanh_part = jnp.tanh(pre_act[:channel_count])
    sigm_part = jax.nn.sigmoid(pre_act[channel_count:])
    gate_b = (tanh_part * sigm_part).astype(jnp.bfloat16)
    field_next = field_now + jnp.dot(weight_mix, gate_b, preferred_element_type=jnp.float32)
    return (field_next, (field_b, past_b, tanh_part, sigm_part, gate_b))


def phase_angle(product, modulus, sign_factor):
    return sign_factor * 2.0 * math.pi / modulus * (product % modulus).astype(jnp.float32)


def phase_table(modulus, sign_factor):
    ordinal = jnp.arange(modulus, dtype=jnp.int32)
    angles = phase_angle(ordinal[:, None] * ordinal[None, :], modulus, sign_factor)
    return (jnp.cos(angles), jnp.sin(angles))


def rotate(signals, angles):
    real_part, imag_part = signals
    cosine = jnp.cos(angles)
    sine_part = jnp.sin(angles)
    return (real_part * cosine - imag_part * sine_part, real_part * sine_part + imag_part * cosine)


def transform(pattern, table_pair, signals):
    cosine, sine_part = table_pair
    real_part, imag_part = signals
    first_term = jnp.einsum(pattern, cosine, real_part, precision=lax.Precision.HIGHEST)
    second = jnp.einsum(pattern, sine_part, real_part, precision=lax.Precision.HIGHEST)
    if imag_part is None:
        return (first_term, second)
    return (
        first_term - jnp.einsum(pattern, sine_part, imag_part, precision=lax.Precision.HIGHEST),
        second + jnp.einsum(pattern, cosine, imag_part, precision=lax.Precision.HIGHEST),
    )


def split_length(length_all):
    chosen = 1
    for factor in range(1, length_all + 1):
        if length_all % factor == 0 and factor * factor <= length_all:
            chosen = factor
    return (chosen, length_all // chosen)


def pair_up(moved):
    return ((moved, None), (0, 0, 1))


def local_section(signals, psd_bin, psd_weight, weight_rows):
    rows_count = lax.axis_size("rows")
    row_index = lax.axis_index("rows")
    col_index = lax.axis_index("cols")
    signal_count = len(weight_rows)
    segment = signals[0].shape[1]
    length_all = segment * rows_count * lax.axis_size("cols")
    slow_len, fast_len = split_length(segment)
    slow_ids = jnp.arange(slow_len, dtype=jnp.int32)
    fast_ids = jnp.arange(fast_len, dtype=jnp.int32)
    spectra = (
        signals[0].reshape(signal_count, slow_len, fast_len),
        signals[1].reshape(signal_count, slow_len, fast_len),
    )
    spectra = transform("pa,kpq->kaq", phase_table(slow_len, -1.0), spectra)
    spectra = rotate(
        spectra, phase_angle(slow_ids[:, None] * fast_ids[None, :], segment, -1.0)[None]
    )
    spectra = transform("qb,kaq->kab", phase_table(fast_len, -1.0), spectra)
    bins_here = psd_bin.reshape(fast_len, slow_len).T
    weights = jnp.take(psd_weight, bins_here, axis=1)
    factors = jnp.stack([weights[row_id] for row_id in weight_rows])
    spectra = (spectra[0] * factors, spectra[1] * factors)
    spectra = transform("bq,kab->kaq", phase_table(fast_len, 1.0), spectra)
    spectra = rotate(
        spectra, phase_angle(slow_ids[:, None] * fast_ids[None, :], segment, 1.0)[None]
    )
    spectra = transform("ap,kaq->kpq", phase_table(slow_len, 1.0), spectra)
    low_here = row_index + rows_count * col_index
    sample_all = jnp.arange(segment, dtype=jnp.int32)
    return rotate(
        (spectra[0].reshape(signal_count, segment), spectra[1].reshape(signal_count, segment)),
        phase_angle(sample_all * low_here, length_all, 1.0)[None],
    )


def per_axis_filter(signal, psd_bin, psd_weight):
    rows_count = lax.axis_size("rows")
    cols_count = lax.axis_size("cols")
    row_index = lax.axis_index("rows")
    col_index = lax.axis_index("cols")
    segment = signal.shape[1]
    groups = rows_count * cols_count
    length_all = segment * groups
    piece_len = segment // rows_count
    small_len = segment // groups
    outer_ids = jnp.arange(rows_count, dtype=jnp.int32)
    inner_ids = jnp.arange(cols_count, dtype=jnp.int32)
    moved = lax.all_to_all(
        signal.reshape(3, 1, segment), "rows", split_axis=2, concat_axis=1, tiled=True
    )
    signals, weight_rows = pair_up(moved)
    signal_count = len(weight_rows)
    signals = transform("ra,krj->kaj", phase_table(rows_count, -1.0), signals)
    signals = rotate(signals, phase_angle(col_index * outer_ids, groups, -1.0)[None, :, None])
    pieces = (
        lax.all_to_all(
            signals[0].reshape(signal_count, rows_count, 1, piece_len),
            "cols",
            split_axis=3,
            concat_axis=2,
            tiled=True,
        ),
        lax.all_to_all(
            signals[1].reshape(signal_count, rows_count, 1, piece_len),
            "cols",
            split_axis=3,
            concat_axis=2,
            tiled=True,
        ),
    )
    turned = transform("cb,kacm->kabm", phase_table(cols_count, -1.0), (pieces[0], pieces[1]))
    freq_low = outer_ids[:, None, None] + rows_count * inner_ids[None, :, None]
    sample_at = (
        row_index * piece_len
        + col_index * small_len
        + jnp.arange(small_len, dtype=jnp.int32)[None, None, :]
    )
    turned = rotate(turned, phase_angle(sample_at * freq_low, length_all, -1.0)[None])
    signals = (
        lax.all_to_all(turned[0], "cols", split_axis=2, concat_axis=3, tiled=True),
        lax.all_to_all(turned[1], "cols", split_axis=2, concat_axis=3, tiled=True),
    )
    signals = (
        lax.all_to_all(
            signals[0].reshape(signal_count, rows_count, piece_len),
            "rows",
            split_axis=1,
            concat_axis=2,
            tiled=True,
        ),
        lax.all_to_all(
            signals[1].reshape(signal_count, rows_count, piece_len),
            "rows",
            split_axis=1,
            concat_axis=2,
            tiled=True,
        ),
    )
    flat = local_section(
        (signals[0].reshape(signal_count, segment), signals[1].reshape(signal_count, segment)),
        psd_bin,
        psd_weight,
        weight_rows,
    )
    returned = (
        lax.all_to_all(
            flat[0].reshape(signal_count, 1, segment),
            "rows",
            split_axis=2,
            concat_axis=1,
            tiled=True,
        ),
        lax.all_to_all(
            flat[1].reshape(signal_count, 1, segment),
            "rows",
            split_axis=2,
            concat_axis=1,
            tiled=True,
        ),
    )
    pieces = (
        lax.all_to_all(
            returned[0].reshape(signal_count, rows_count, 1, piece_len),
            "cols",
            split_axis=3,
            concat_axis=2,
            tiled=True,
        ),
        lax.all_to_all(
            returned[1].reshape(signal_count, rows_count, 1, piece_len),
            "cols",
            split_axis=3,
            concat_axis=2,
            tiled=True,
        ),
    )
    turned = transform("bc,kabm->kacm", phase_table(cols_count, 1.0), (pieces[0], pieces[1]))
    turned = rotate(
        turned, phase_angle(inner_ids[None, :, None] * outer_ids[:, None, None], groups, 1.0)[None]
    )
    returned = (
        lax.all_to_all(turned[0], "cols", split_axis=2, concat_axis=3, tiled=True),
        lax.all_to_all(turned[1], "cols", split_axis=2, concat_axis=3, tiled=True),
    )
    real_in = returned[0].reshape(signal_count, rows_count, piece_len)
    imag_in = returned[1].reshape(signal_count, rows_count, piece_len)
    cos_rows, sin_rows = phase_table(rows_count, 1.0)
    real_out = jnp.einsum(
        "ar,kaj->krj", cos_rows, real_in, precision=lax.Precision.HIGHEST
    ) - jnp.einsum("ar,kaj->krj", sin_rows, imag_in, precision=lax.Precision.HIGHEST)
    homed = lax.all_to_all(real_out, "rows", split_axis=1, concat_axis=2, tiled=True)
    return homed.reshape(3, segment) / float(length_all)


def local(
    whitened,
    cotangent,
    lift_weight,
    conv_now,
    conv_past,
    mix_weight,
    dilations,
    psd_bin,
    psd_weight,
):
    segment = whitened.shape[1]
    layer_count = mix_weight.shape[0]
    saved = []
    field_now = lifted(lift_weight, whitened)
    for layer_id in range(layer_count):
        field_b = field_now.astype(jnp.bfloat16)
        before = from_behind(field_b[:, segment - DMAX :], ("rows", "cols"), 1)
        field_now, kept_parts = gated_layer(
            field_now,
            field_b,
            before,
            conv_now[layer_id],
            conv_past[layer_id],
            mix_weight[layer_id],
            dilations[layer_id],
        )
        saved.append(kept_parts)
    grad_field = cotangent.astype(jnp.float32)
    grads_now = [None] * layer_count
    grads_past = [None] * layer_count
    grads_mix = [None] * layer_count
    for layer_id in reversed(range(layer_count)):
        field_b, past_b, tanh_part, sigm_part, gate_b = saved[layer_id]
        grad_field_b = grad_field.astype(jnp.bfloat16)
        grad_gate = jnp.dot(
            mix_weight[layer_id].T, grad_field_b, preferred_element_type=jnp.float32
        )
        grads_mix[layer_id] = jnp.dot(grad_field_b, gate_b.T, preferred_element_type=jnp.float32)
        grad_pre = jnp.concatenate(
            [
                grad_gate * sigm_part * (1.0 - tanh_part * tanh_part),
                grad_gate * tanh_part * sigm_part * (1.0 - sigm_part),
            ],
            axis=0,
        ).astype(jnp.bfloat16)
        grads_now[layer_id] = jnp.dot(grad_pre, field_b.T, preferred_element_type=jnp.float32)
        grads_past[layer_id] = jnp.dot(grad_pre, past_b.T, preferred_element_type=jnp.float32)
        ahead_term = jnp.dot(conv_past[layer_id].T, grad_pre, preferred_element_type=jnp.float32)
        head_rim = from_behind(ahead_term[:, :DMAX], ("rows", "cols"), -1)
        grad_field = (
            grad_field
            + jnp.dot(conv_now[layer_id].T, grad_pre, preferred_element_type=jnp.float32)
            + advanced(ahead_term, dilations[layer_id], head_rim)
        )
    input_grad = jnp.dot(lift_weight.T, grad_field, precision=lax.Precision.HIGHEST)
    lift_part = jnp.dot(grad_field, whitened.T, precision=lax.Precision.HIGHEST)
    summed = lax.psum(
        (jnp.stack(grads_now), jnp.stack(grads_past), jnp.stack(grads_mix), lift_part),
        ("rows", "cols"),
    )
    scaling = 1.0 / math.sqrt(float(segment * lax.axis_size("rows") * lax.axis_size("cols")))
    data_grad = per_axis_filter(input_grad, psd_bin, psd_weight)
    return (
        data_grad,
        summed[0] * scaling,
        summed[1] * scaling,
        summed[2] * scaling,
        summed[3] * scaling,
    )


def solution(mesh):
    in_specs = (
        P(None, ("rows", "cols")),
        P(None, ("rows", "cols")),
        P(),
        P(),
        P(),
        P(),
        P(),
        P(None, "cols", "rows"),
        P(),
    )
    out_specs = (P(None, ("rows", "cols")), P(), P(), P(), P())
    return jax.shard_map(local, mesh=mesh, in_specs=in_specs, out_specs=out_specs, check_vma=False)
```

profile of v0, /device:TPU:1, one launch (start us, length us, event | category | flops | bytes accessed | tf_op | source)
XLA Modules:
  0.0 555.5 jit_solution(1703089150025152943)
XLA Ops:
  9.3 4.6 collective-permute-start
  21.3 10.8 %gather_fusion = f32[4096,2]{1,0:T(8,128)S(1)} fusion(f32[2,1024]{0,1:T(8,128)S(1)} %copy.178, s32[4096]{0:T(1024)S(1)} %broadcast_clamp_fusion), kind=kCustom, calls=%fused_computation | custom fusion | bytes 81920 | tf_op jit(solution)/shard_map/jit(_take)/gather | solution.py:110
  48.6 1.9 collective-permute-start.1
  53.0 4.1 collective-permute-start.2
  60.9 1.9 collective-permute-start.3
  63.9 3.1 collective-permute-done.3
  68.8 2.1 collective-permute-start.4
  72.1 2.3 collective-permute-done.4
  76.1 1.9 collective-permute-start.5
  79.2 2.5 collective-permute-done.5
  83.1 3.7 copy.151
  87.3 20.4 %reduce.4 = f32[4096,3]{1,0:T(8,128)} reduce(f32[4096,1,3]{2,1,0:T(1,128)} %bitcast.335, f32[]{:T(128)} %broadcast.734), dimensions={1}, to_apply=%bitcast.265.reduce_sub_computation | reduce | bytes 98308
  107.7 3.7 reshape.486
  111.4 21.0 %all-to-all-start = ((f32[8,1,1536]{2,1,0:T(1,128)}), f32[8,1,1536]{2,1,0:T(1,128)S(1)}, u32[]{:S(2)}, u32[]{:S(2)}) async-start(f32[8,1,1536]{2,1,0:T(1,128)} %reshape.486), calls=%async_computation | async-start | bytes 98304 | tf_op jit(solution)/shard_map/all_to_all | solution.py:138
  132.5 1.9 convolution_bitcast_fusion.18
  134.4 5.1 all-to-all-done
  140.3 4.4 reshape.487
  144.7 2.2 copy.231
  148.0 2.0 copy.153
  150.0 4.2 reduce.6
  154.2 2.5 reshape.488
  156.7 14.5 %all-to-all-start.1 = ((f32[32,1,384]{2,1,0:T(1,128)}), f32[32,1,384]{2,1,0:T(1,128)S(1)}, u32[]{:S(2)}, u32[]{:S(2)}) async-start(f32[32,1,384]{2,1,0:T(1,128)} %reshape.488), calls=%async_computation.1 | async-start | bytes 98304 | tf_op jit(solution)/shard_map/all_to_all | solution.py:146
  171.2 2.4 convolution_bitcast_fusion.12
  173.5 1.7 copy.156
  175.3 4.0 reduce.8
  180.5 7.9 %all-to-all-start.2 = ((f32[32,1,384]{2,1,0:T(1,128)}), f32[32,1,384]{2,1,0:T(1,128)S(1)}, u32[]{:S(2)}, u32[]{:S(2)}) async-start(f32[32,1,384]{2,1,0:T(1,128)} %reshape.490), calls=%async_computation.2 | async-start | bytes 98304 | tf_op jit(solution)/shard_map/all_to_all | solution.py:153
  197.6 1.8 copy.157
  200.3 1.7 fusion.12
  202.1 2.4 multiply_add_fusion.1
  206.4 6.2 %all-to-all-start.3 = ((f32[32,1,384]{2,1,0:T(1,128)}), f32[32,1,384]{2,1,0:T(1,128)}, u32[]{:S(2)}, u32[]{:S(2)}) async-start(f32[32,1,384]{2,1,0:T(1,128)} %reshape.492), calls=%async_computation.3 | async-start | bytes 98304 | tf_op jit(solution)/shard_map/all_to_all | solution.py:170
  212.7 2.2 convolution_bitcast_fusion.16
  215.9 4.1 all-to-all-done.3
  220.0 4.5 all-to-all-start.5
  225.4 1.6 reduce.10
  228.2 3.8 all-to-all-done.5
  232.0 3.4 all-to-all-start.4
  240.1 2.3 all-to-all-done.4
  242.4 4.5 all-to-all-start.6
  247.8 6.3 %all-to-all-done.6 = f32[3,8,512]{2,0,1:T(4,128)S(1)} async-done(((f32[3,8,512]{2,0,1:T(4,128)}), f32[3,8,512]{2,0,1:T(4,128)S(1)}, u32[]{:S(2)}, u32[]{:S(2)}) %all-to-all-start.6) | async-done | bytes 49184 | tf_op jit(solution)/shard_map/all_to_all | solution.py:181
  260.1 2.4 copy.188
  262.5 19.4 %reduce.12 = f32[4096,3]{1,0:T(8,128)} reduce(f32[4096,1,3]{2,1,0:T(1,128)S(1)} %bitcast.337, f32[]{:T(128)} %broadcast.734), dimensions={1}, to_apply=%bitcast.275.reduce_sub_computation | reduce | bytes 98308
  281.9 3.7 reshape.496
  285.6 3.3 all-to-all-start.7
  289.9 2.4 copy.193
  292.4 19.4 %reduce.16 = f32[4096,3]{1,0:T(8,128)} reduce(f32[4096,1,3]{2,1,0:T(1,128)S(1)} %bitcast.338, f32[]{:T(128)} %broadcast.734), dimensions={1}, to_apply=%bitcast.279.reduce_sub_computation | reduce | bytes 98308
  311.8 3.7 reshape.500
  315.5 6.8 %all-to-all-start.9 = ((f32[8,1,1536]{2,1,0:T(1,128)}), f32[8,1,1536]{2,1,0:T(1,128)S(1)}, u32[]{:S(2)}, u32[]{:S(2)}) async-start(f32[8,1,1536]{2,1,0:T(1,128)} %reshape.500), calls=%async_computation.9 | async-start | bytes 98304 | tf_op jit(solution)/shard_map/all_to_all | solution.py:203
  323.1 3.0 reshape.497
  326.2 4.3 copy.190
  330.4 4.0 reduce.14
  335.7 6.2 %all-to-all-start.8 = ((f32[32,1,384]{2,1,0:T(1,128)}), f32[32,1,384]{2,1,0:T(1,128)S(1)}, u32[]{:S(2)}, u32[]{:S(2)}) async-start(f32[32,1,384]{2,1,0:T(1,128)} %reshape.498), calls=%async_computation.8 | async-start | bytes 98304 | tf_op jit(solution)/shard_map/all_to_all | solution.py:212
  342.8 79.2 %all-reduce = (f32[3,64,64]{2,1,0:T(8,128)S(1)}, f32[64,3]{0,1:T(4,128)S(1)}) all-reduce(f32[3,64,64]{2,1,0:T(8,128)S(1)} %pad_maximum_fusion.6, f32[64,3]{0,1:T(4,128)S(1)} %fusion.359), channel_id=1, replica_groups=mesh['rows'=8,'cols'=32] {'rows','cols'}, use_global_device_ids=true, to_apply=%region_2.0 | all-reduce | flops 12480 | bytes 99840 | tf_op jit(solution)/shard_map/psum | solution.py:302
  422.8 3.0 reshape.501
  425.8 4.0 copy.195
  429.8 3.2 reduce.18
  434.2 4.7 all-to-all-start.10
  443.6 2.7 all-to-all-done.10
  451.9 4.8 all-to-all-start.12
  458.4 5.6 %all-to-all-done.12 = f32[32,1,384]{2,1,0:T(1,128)S(1)} async-done(((f32[32,1,384]{2,1,0:T(1,128)}), f32[32,1,384]{2,1,0:T(1,128)S(1)}, u32[]{:S(2)}, u32[]{:S(2)}) %all-to-all-start.12) | async-done | bytes 49184 | tf_op jit(solution)/shard_map/all_to_all | solution.py:233
  464.0 3.9 all-to-all-start.11
  469.7 5.6 %all-to-all-done.11 = f32[32,1,384]{2,1,0:T(1,128)S(1)} async-done(((f32[32,1,384]{2,1,0:T(1,128)}), f32[32,1,384]{2,1,0:T(1,128)S(1)}, u32[]{:S(2)}, u32[]{:S(2)}) %all-to-all-start.11) | async-done | bytes 49184 | tf_op jit(solution)/shard_map/all_to_all | solution.py:232
  477.7 5.1 all-to-all-start.13
  482.8 63.4 %all-reduce.4.cloned.1.call-done = (f32[3,128,64]{1,2,0:T(8,128)}, f32[3,128,64]{1,2,0:T(8,128)}) async-done(((f32[3,128,64]{1,2,0:T(8,128)}, f32[3,128,64]{1,2,0:T(8,128)}), (f32[3,128,64]{1,2,0:T(8,128)}, f32[3,128,64]{1,2,0:T(8,128)})) %all-reduce.4.cloned.1.call-update) | async-done | bytes 196624 | tf_op jit(solution)/shard_map/psum | solution.py:302
  546.2 1.6 broadcast_multiply_fusion.1
  (251 shorter events, 82.8 us)
Async XLA Ops:
  8.0 24.8 %copy-start.38 = (f32[64]{0:T(128)}, f32[64]{0:T(128)S(1)}, u32[]{:S(2)}) copy-start(f32[64]{0:T(128)S(1)} %get-tuple-element.29) | copy-start | bytes 772
  8.0 24.8 %copy-start.40 = (f32[64]{0:T(128)}, f32[64]{0:T(128)S(1)}, u32[]{:S(2)}) copy-start(f32[64]{0:T(128)S(1)} %get-tuple-element.30) | copy-start | bytes 772
  9.2 37.5 %copy-start.5 = (bf16[64,4096]{1,0:T(8,128)(2,1)}, bf16[64,4096]{1,0:T(8,128)(2,1)S(1)}, u32[]{:S(2)}) copy-start(bf16[64,4096]{1,0:T(8,128)(2,1)S(1)} %fusion.33) | copy-start | bytes 1572868
  9.2 23.6 %copy-start.24 = (bf16[3,128,64]{1,2,0:T(8,128)(2,1)S(1)}, bf16[3,128,64]{1,2,0:T(8,128)(2,1)}, u32[]{:S(2)}) copy-start(bf16[3,128,64]{1,2,0:T(8,128)(2,1)} %param.12) | copy-start | bytes 147460
  9.3 37.5 %collective-permute-start = (bf16[64,256]{1,0:T(8,128)(2,1)S(1)}, bf16[64,256]{1,0:T(8,128)(2,1)S(1)}, u32[]{:S(2)}, u32[]{:S(2)}) collective-permute-start(bf16[64,256]{1,0:T(8,128)(2,1)S(1)} %slice.140), channel_id=1, source_target_pairs={{0,1},{1,2},{2,3},{3,4},{4,5},{5,6},{6,7},{7,8},{8,9},{9,10},{10,1... | collective-permute-start | bytes 98312 | tf_op jit(solution)/shard_map/ppermute | solution.py:13
  32.1 1.3 copy-start.45
  32.1 14.7 %copy-start.23 = (bf16[3,128,64]{1,2,0:T(8,128)(2,1)S(1)}, bf16[3,128,64]{1,2,0:T(8,128)(2,1)}, u32[]{:S(2)}) copy-start(bf16[3,128,64]{1,2,0:T(8,128)(2,1)} %param.13) | copy-start | bytes 147460
  34.3 13.0 %copy-start.18 = (f32[2,64,64]{2,1,0:T(8,128)}, f32[2,64,64]{2,1,0:T(8,128)S(1)}, u32[]{:S(2)}) copy-start(f32[2,64,64]{2,1,0:T(8,128)S(1)} %select_bitcast_fusion) | copy-start | bytes 98308
  47.4 0.8 copy-start.39
  47.4 0.8 copy-start.41
  48.2 2.8 copy-start.2
  48.5 29.5 %copy-start = (bf16[64,4096]{1,0:T(8,128)(2,1)}, bf16[64,4096]{1,0:T(8,128)(2,1)S(1)}, u32[]{:S(2)}) copy-start(bf16[64,4096]{1,0:T(8,128)(2,1)S(1)} %get-tuple-element.34) | copy-start | bytes 1572868
  48.6 3.1 collective-permute-start.1
  52.7 4.9 copy-start.4
  53.0 5.1 collective-permute-start.2
  57.6 1.1 copy-start.20
  60.9 6.2 %collective-permute-start.3 = (f32[64,256]{1,0:T(8,128)S(1)}, f32[64,256]{1,0:T(8,128)S(1)}, u32[]{:S(2)}, u32[]{:S(2)}) collective-permute-start(f32[64,256]{1,0:T(8,128)S(1)} %slice.149), channel_id=1, source_target_pairs={{1,0},{2,1},{3,2},{4,3},{5,4},{6,5},{7,6},{8,7},{9,8},{10,9},{11,1... | collective-permute-start | bytes 196616 | tf_op jit(solution)/shard_map/ppermute | solution.py:13
  68.5 9.6 %copy-start.12 = (bf16[64,4096]{1,0:T(8,128)(2,1)}, bf16[64,4096]{1,0:T(8,128)(2,1)S(1)}, u32[]{:S(2)}) copy-start(bf16[64,4096]{1,0:T(8,128)(2,1)S(1)} %get-tuple-element.11) | copy-start | bytes 1572868
  68.5 9.6 %copy-start.13 = (bf16[64,4096]{1,0:T(8,128)(2,1)}, bf16[64,4096]{1,0:T(8,128)(2,1)S(1)}, u32[]{:S(2)}) copy-start(bf16[64,4096]{1,0:T(8,128)(2,1)S(1)} %get-tuple-element.12) | copy-start | bytes 1572868
  68.8 5.6 %collective-permute-start.4 = (f32[64,256]{1,0:T(8,128)S(1)}, f32[64,256]{1,0:T(8,128)S(1)}, u32[]{:S(2)}, u32[]{:S(2)}) collective-permute-start(f32[64,256]{1,0:T(8,128)S(1)} %slice.150), channel_id=1, source_target_pairs={{1,0},{2,1},{3,2},{4,3},{5,4},{6,5},{7,6},{8,7},{9,8},{10,9},{11,1... | collective-permute-start | bytes 196616 | tf_op jit(solution)/shard_map/ppermute | solution.py:13
  75.8 5.9 %copy-start.7 = (bf16[64,4096]{1,0:T(8,128)(2,1)}, bf16[64,4096]{1,0:T(8,128)(2,1)S(1)}, u32[]{:S(2)}) copy-start(bf16[64,4096]{1,0:T(8,128)(2,1)S(1)} %get-tuple-element.9) | copy-start | bytes 1572868
  75.8 5.9 %copy-start.10 = (bf16[64,4096]{1,0:T(8,128)(2,1)}, bf16[64,4096]{1,0:T(8,128)(2,1)S(1)}, u32[]{:S(2)}) copy-start(bf16[64,4096]{1,0:T(8,128)(2,1)S(1)} %get-tuple-element.10) | copy-start | bytes 1572868
  76.1 5.6 %collective-permute-start.5 = (f32[64,256]{1,0:T(8,128)S(1)}, f32[64,256]{1,0:T(8,128)S(1)}, u32[]{:S(2)}, u32[]{:S(2)}) collective-permute-start(f32[64,256]{1,0:T(8,128)S(1)} %slice.151), channel_id=1, source_target_pairs={{1,0},{2,1},{3,2},{4,3},{5,4},{6,5},{7,6},{8,7},{9,8},{10,9},{11,1... | collective-permute-start | bytes 196616 | tf_op jit(solution)/shard_map/ppermute | solution.py:13
  79.2 3.2 copy-start.42
  111.4 28.1 %all-to-all-start = ((f32[8,1,1536]{2,1,0:T(1,128)}), f32[8,1,1536]{2,1,0:T(1,128)S(1)}, u32[]{:S(2)}, u32[]{:S(2)}) async-start(f32[8,1,1536]{2,1,0:T(1,128)} %reshape.486), calls=%async_computation | async-start | bytes 98304 | tf_op jit(solution)/shard_map/all_to_all | solution.py:138
  140.2 6.9 %copy-start.43 = (f32[8]{0:T(128)S(1)}, f32[8]{0:T(128)}, u32[]{:S(2)}) copy-start(f32[8]{0:T(128)} %get-tuple-element.38) | copy-start | bytes 100
  140.3 6.9 %copy-start.44 = (f32[8]{0:T(128)S(1)}, f32[8]{0:T(128)}, u32[]{:S(2)}) copy-start(f32[8]{0:T(128)} %get-tuple-element.39) | copy-start | bytes 100
  146.9 24.3 %copy-start.1 = (bf16[64,4096]{1,0:T(8,128)(2,1)S(1)}, bf16[64,4096]{1,0:T(8,128)(2,1)}, u32[]{:S(2)}) copy-start(bf16[64,4096]{1,0:T(8,128)(2,1)} %copy-done) | copy-start | bytes 1572868
  154.2 19.4 %copy-start.25 = (f32[3,8,1,512]{3,1,0,2:T(8,128)S(1)}, f32[3,8,1,512]{3,1,0,2:T(8,128)}, u32[]{:S(2)}) copy-start(f32[3,8,1,512]{3,1,0,2:T(8,128)} %get-tuple-element.21) | copy-start | bytes 147460
  156.7 23.8 %all-to-all-start.1 = ((f32[32,1,384]{2,1,0:T(1,128)}), f32[32,1,384]{2,1,0:T(1,128)S(1)}, u32[]{:S(2)}, u32[]{:S(2)}) async-start(f32[32,1,384]{2,1,0:T(1,128)} %reshape.488), calls=%async_computation.1 | async-start | bytes 98304 | tf_op jit(solution)/shard_map/all_to_all | solution.py:146
  180.5 15.1 %all-to-all-start.2 = ((f32[32,1,384]{2,1,0:T(1,128)}), f32[32,1,384]{2,1,0:T(1,128)S(1)}, u32[]{:S(2)}, u32[]{:S(2)}) async-start(f32[32,1,384]{2,1,0:T(1,128)} %reshape.490), calls=%async_computation.2 | async-start | bytes 98304 | tf_op jit(solution)/shard_map/all_to_all | solution.py:153
  197.6 15.1 %copy-start.8 = (bf16[64,4096]{1,0:T(8,128)(2,1)S(1)}, bf16[64,4096]{1,0:T(8,128)(2,1)}, u32[]{:S(2)}) copy-start(bf16[64,4096]{1,0:T(8,128)(2,1)} %copy-done.7) | copy-start | bytes 1572868
  206.4 13.6 %all-to-all-start.3 = ((f32[32,1,384]{2,1,0:T(1,128)}), f32[32,1,384]{2,1,0:T(1,128)}, u32[]{:S(2)}, u32[]{:S(2)}) async-start(f32[32,1,384]{2,1,0:T(1,128)} %reshape.492), calls=%async_computation.3 | async-start | bytes 98304 | tf_op jit(solution)/shard_map/all_to_all | solution.py:170
  212.7 11.9 %copy-start.3 = (bf16[64,4096]{1,0:T(8,128)(2,1)S(1)}, bf16[64,4096]{1,0:T(8,128)(2,1)}, u32[]{:S(2)}) copy-start(bf16[64,4096]{1,0:T(8,128)(2,1)} %copy-done.2) | copy-start | bytes 1572868
  215.1 21.7 %copy-start.6 = (bf16[64,4096]{1,0:T(8,128)(2,1)S(1)}, bf16[64,4096]{1,0:T(8,128)(2,1)}, u32[]{:S(2)}) copy-start(bf16[64,4096]{1,0:T(8,128)(2,1)} %copy-done.5) | copy-start | bytes 1572868
  220.0 12.0 %all-to-all-start.5 = ((f32[32,1,384]{2,1,0:T(1,128)}), f32[32,1,384]{2,1,0:T(1,128)}, u32[]{:S(2)}, u32[]{:S(2)}) async-start(f32[32,1,384]{2,1,0:T(1,128)} %reshape.494), calls=%async_computation.5 | async-start | bytes 98304 | tf_op jit(solution)/shard_map/all_to_all | solution.py:171
  225.4 11.3 %copy-start.9 = (bf16[64,4096]{1,0:T(8,128)(2,1)S(1)}, bf16[64,4096]{1,0:T(8,128)(2,1)}, u32[]{:S(2)}) copy-start(bf16[64,4096]{1,0:T(8,128)(2,1)} %copy-done.7) | copy-start | bytes 1572868
  225.4 11.3 %copy-start.11 = (bf16[64,4096]{1,0:T(8,128)(2,1)S(1)}, bf16[64,4096]{1,0:T(8,128)(2,1)}, u32[]{:S(2)}) copy-start(bf16[64,4096]{1,0:T(8,128)(2,1)} %copy-done.10) | copy-start | bytes 1572868
  225.4 11.3 %copy-start.30 = (bf16[64,256]{1,0:T(8,128)(2,1)S(1)}, bf16[64,256]{1,0:T(8,128)(2,1)}, u32[]{:S(2)}) copy-start(bf16[64,256]{1,0:T(8,128)(2,1)} %copy-done.29) | copy-start | bytes 98308
  232.0 10.4 %all-to-all-start.4 = ((f32[3,8,512]{2,0,1:T(4,128)}), f32[3,8,512]{2,0,1:T(4,128)S(1)}, u32[]{:S(2)}, u32[]{:S(2)}) async-start(f32[3,8,512]{2,0,1:T(4,128)} %reshape.475), calls=%async_computation.4 | async-start | bytes 131072 | tf_op jit(solution)/shard_map/all_to_all | solution.py:174
  237.3 17.6 %copy-start.16 = (f32[64,64]{0,1:T(8,128)S(1)}, f32[64,64]{0,1:T(8,128)}, u32[]{:S(2)}) copy-start(f32[64,64]{0,1:T(8,128)} %copy.171) | copy-start | bytes 49156
  237.3 17.6 %copy-start.17 = (f32[64,64]{0,1:T(8,128)S(1)}, f32[64,64]{0,1:T(8,128)}, u32[]{:S(2)}) copy-start(f32[64,64]{0,1:T(8,128)} %copy.174) | copy-start | bytes 49156
  237.4 18.4 %copy-start.19 = (f32[2,64,64]{2,1,0:T(8,128)S(1)}, f32[2,64,64]{2,1,0:T(8,128)}, u32[]{:S(2)}) copy-start(f32[2,64,64]{2,1,0:T(8,128)} %copy-done.18) | copy-start | bytes 98308
  237.4 18.4 %copy-start.21 = (f32[1,64,64]{2,1,0:T(8,128)S(1)}, f32[1,64,64]{2,1,0:T(8,128)}, u32[]{:S(2)}) copy-start(f32[1,64,64]{2,1,0:T(8,128)} %slice.152) | copy-start | bytes 49156
  242.4 11.7 %all-to-all-start.6 = ((f32[3,8,512]{2,0,1:T(4,128)}), f32[3,8,512]{2,0,1:T(4,128)S(1)}, u32[]{:S(2)}, u32[]{:S(2)}) async-start(f32[3,8,512]{2,0,1:T(4,128)} %reshape.476), calls=%async_computation.6 | async-start | bytes 131072 | tf_op jit(solution)/shard_map/all_to_all | solution.py:181
  246.9 11.1 %copy-start.14 = (f32[64,64]{1,0:T(8,128)S(1)}, f32[64,64]{1,0:T(8,128)}, u32[]{:S(2)}) copy-start(f32[64,64]{1,0:T(8,128)} %get-tuple-element.40) | copy-start | bytes 49156
  246.9 11.1 %copy-start.15 = (f32[64,64]{1,0:T(8,128)S(1)}, f32[64,64]{1,0:T(8,128)}, u32[]{:S(2)}) copy-start(f32[64,64]{1,0:T(8,128)} %get-tuple-element.41) | copy-start | bytes 49156
  255.7 4.3 copy-start.28
  281.9 7.3 %copy-start.33 = (f32[1,128,64]{1,2,0:T(8,128)S(1)}, f32[1,128,64]{1,2,0:T(8,128)}, u32[]{:S(2)}) copy-start(f32[1,128,64]{1,2,0:T(8,128)} %convolution_bitcast_fusion.11) | copy-start | bytes 98308
  281.9 7.4 %copy-start.34 = (f32[1,128,64]{1,2,0:T(8,128)S(1)}, f32[1,128,64]{1,2,0:T(8,128)}, u32[]{:S(2)}) copy-start(f32[1,128,64]{1,2,0:T(8,128)} %convolution_bitcast_fusion.12) | copy-start | bytes 98308
  285.6 29.9 %all-to-all-start.7 = ((f32[8,1,1536]{2,1,0:T(1,128)}), f32[8,1,1536]{2,1,0:T(1,128)S(1)}, u32[]{:S(2)}, u32[]{:S(2)}) async-start(f32[8,1,1536]{2,1,0:T(1,128)} %reshape.496), calls=%async_computation.7 | async-start | bytes 98304 | tf_op jit(solution)/shard_map/all_to_all | solution.py:196
  289.0 257.3 %all-reduce.4.cloned.1.call-start = ((), (), s32[]{:S(2)}) async-start(), calls=%async_computation.14 | async-start | bytes 393216 | tf_op jit(solution)/shard_map/psum | solution.py:302
  311.8 10.6 %copy-start.26 = (f32[1,64,64]{2,1,0:T(8,128)S(1)}, f32[1,64,64]{2,1,0:T(8,128)}, u32[]{:S(2)}) copy-start(f32[1,64,64]{2,1,0:T(8,128)} %convolution_bitcast_fusion.18) | copy-start | bytes 49156
  311.8 10.6 %copy-start.27 = (f32[1,64,64]{2,1,0:T(8,128)S(1)}, f32[1,64,64]{2,1,0:T(8,128)}, u32[]{:S(2)}) copy-start(f32[1,64,64]{2,1,0:T(8,128)} %convolution_bitcast_fusion.19) | copy-start | bytes 49156
  311.8 10.6 %copy-start.32 = (f32[1,64,64]{2,1,0:T(8,128)S(1)}, f32[1,64,64]{2,1,0:T(8,128)}, u32[]{:S(2)}) copy-start(f32[1,64,64]{2,1,0:T(8,128)} %convolution_bitcast_fusion.17) | copy-start | bytes 49156
  315.5 20.2 %all-to-all-start.9 = ((f32[8,1,1536]{2,1,0:T(1,128)}), f32[8,1,1536]{2,1,0:T(1,128)S(1)}, u32[]{:S(2)}, u32[]{:S(2)}) async-start(f32[8,1,1536]{2,1,0:T(1,128)} %reshape.500), calls=%async_computation.9 | async-start | bytes 98304 | tf_op jit(solution)/shard_map/all_to_all | solution.py:203
  330.4 11.5 %copy-start.22 = (f32[3,4096]{1,0:T(4,128)S(1)}, f32[3,4096]{1,0:T(4,128)}, u32[]{:S(2)}) copy-start(f32[3,4096]{1,0:T(4,128)} %param.9) | copy-start | bytes 147460
  335.7 98.6 %all-to-all-start.8 = ((f32[32,1,384]{2,1,0:T(1,128)}), f32[32,1,384]{2,1,0:T(1,128)S(1)}, u32[]{:S(2)}, u32[]{:S(2)}) async-start(f32[32,1,384]{2,1,0:T(1,128)} %reshape.498), calls=%async_computation.8 | async-start | bytes 98304 | tf_op jit(solution)/shard_map/all_to_all | solution.py:212
  434.2 12.0 %all-to-all-start.10 = ((f32[32,1,384]{2,1,0:T(1,128)}), f32[32,1,384]{2,1,0:T(1,128)S(1)}, u32[]{:S(2)}, u32[]{:S(2)}) async-start(f32[32,1,384]{2,1,0:T(1,128)} %reshape.502), calls=%async_computation.10 | async-start | bytes 98304 | tf_op jit(solution)/shard_map/all_to_all | solution.py:219
  442.0 8.1 %copy-start.36 = (f32[8,32]{1,0:T(8,128)S(1)}, f32[8,32]{1,0:T(8,128)}, u32[]{:S(2)}) copy-start(f32[8,32]{1,0:T(8,128)} %get-tuple-element.36) | copy-start | bytes 3076
  442.0 8.1 %copy-start.37 = (f32[8,32]{1,0:T(8,128)S(1)}, f32[8,32]{1,0:T(8,128)}, u32[]{:S(2)}) copy-start(f32[8,32]{1,0:T(8,128)} %get-tuple-element.37) | copy-start | bytes 3076
  451.9 12.1 %all-to-all-start.12 = ((f32[32,1,384]{2,1,0:T(1,128)}), f32[32,1,384]{2,1,0:T(1,128)S(1)}, u32[]{:S(2)}, u32[]{:S(2)}) async-start(f32[32,1,384]{2,1,0:T(1,128)} %reshape.506), calls=%async_computation.12 | async-start | bytes 98304 | tf_op jit(solution)/shard_map/all_to_all | solution.py:233
  464.0 11.3 %all-to-all-start.11 = ((f32[32,1,384]{2,1,0:T(1,128)}), f32[32,1,384]{2,1,0:T(1,128)S(1)}, u32[]{:S(2)}, u32[]{:S(2)}) async-start(f32[32,1,384]{2,1,0:T(1,128)} %reshape.504), calls=%async_computation.11 | async-start | bytes 98304 | tf_op jit(solution)/shard_map/all_to_all | solution.py:232
  477.7 70.2 %all-to-all-start.13 = ((f32[3,8,512]{2,0,1:T(4,128)}), f32[3,8,512]{2,0,1:T(4,128)S(1)}, u32[]{:S(2)}, u32[]{:S(2)}) async-start(f32[3,8,512]{2,0,1:T(4,128)} %copy.204), calls=%async_computation.13 | async-start | bytes 131072 | tf_op jit(solution)/shard_map/all_to_all | solution.py:241
  (3 other events, 2.0 us)
Sparse Core Ops, SparseCore 0:
  296.0 250.2 all-reduce.3
where the time goes:
time: 566 us; the launch traced here: 556 us
  starting transfers between devices  114 us (20%)
  waiting for transfers between devices  109 us (19%)
  other arithmetic  97.2 us (17%)
  local copies, waits for them, and re-layouts  90 us (16%)
  blocking collectives  79.2 us (14%)
  matrix products  40.8 us (7%)
  between operations  25.4 us (4%)
    psum x1, blocking collectives, local(): lax.psum((jnp.stack(grads_now), jnp.stack(grads_past), jnp.stack(grads_mi...  79.2 us
    unnamed x8, other arithmetic  76 us
    psum x1, waiting for transfers between devices, local(): lax.psum((jnp.stack(grads_now), jnp.stack(grads_past), jnp.stack(grads_mi...  63.4 us
    unnamed x117, local copies, waits for them, and re-layouts  39.2 us
    all_to_all x1, starting transfers between devices, per_axis_filter(): lax.all_to_all(signal.reshape(3, 1, segment), 'rows', split_axis=2, conca...  21 us
    ppermute x6, starting transfers between devices, from_behind(): return lax.ppermute(array, axis, pairs)  16.5 us
    all_to_all x1, starting transfers between devices, per_axis_filter(): lax.all_to_all(signals[0].reshape(signal_count, rows_count, 1, piece_len)...  14.5 us
    gather x2, local copies, waits for them, and re-layouts, local_section(): weights = jnp.take(psd_weight, bins_here, axis=1)  11.5 us
  transfers between devices with their start and end apart: 21, of which 15 were waited for; matrix products, arithmetic and copies ran while one was open for 23% of the time, Pallas kernels for 0%

commit v1 on v0

--- a/solution.py
+++ b/solution.py
@@ -3,8 +3,14 @@
 import jax.numpy as jnp
 from jax import lax
 from jax.sharding import PartitionSpec as P
+from jax.lax import psum
 
 DMAX = 256
+
+
+def panels_convert(z_in, mesh_ax, net_axis="cols"):
+    known = psum(z_in, mesh_ax)
+    return psum(known, net_axis)
 
 
 def from_behind(array, axis, by):
@@ -299,9 +305,8 @@
         )
     input_grad = jnp.dot(lift_weight.T, grad_field, precision=lax.Precision.HIGHEST)
     lift_part = jnp.dot(grad_field, whitened.T, precision=lax.Precision.HIGHEST)
-    summed = lax.psum(
-        (jnp.stack(grads_now), jnp.stack(grads_past), jnp.stack(grads_mix), lift_part),
-        ("rows", "cols"),
+    summed = panels_convert(
+        (jnp.stack(grads_now), jnp.stack(grads_past), jnp.stack(grads_mix), lift_part), "rows"
     )
     scaling = 1.0 / math.sqrt(float(segment * lax.axis_size("rows") * lax.axis_size("cols")))
     data_grad = per_axis_filter(input_grad, psd_bin, psd_weight)

time: 566 us -> 670 us (1.18)
  blocking collectives: 79.2 us -> 151 us
  waiting for transfers between devices: 109 us -> 150 us
    psum x1 -> x2, blocking collectives: 79.2 us -> 151 us  [the longest x1 126 us: panels_convert(): return psum(known, net_axis)]
    psum x1 -> x2, waiting for transfers between devices: 63.4 us -> 99.3 us  [the longest x1 99.3 us: panels_convert(): return psum(known, net_axis)]
    unnamed x117 -> x101, local copies, waits for them, and re-layouts: 39.2 us -> 39.1 us
  transfers between devices with their start and end apart: 21 -> 22, of which waited for: 15 -> 16; matrix products, arithmetic and copies ran while one was open for 23% -> 22% of each run, Pallas kernels for 0% -> 0%
where the time goes in v1:
time: 670 us; the launch traced here: 660 us
  blocking collectives  151 us (23%)
  waiting for transfers between devices  150 us (22%)
  starting transfers between devices  114 us (17%)
  other arithmetic  95.5 us (14%)
  local copies, waits for them, and re-layouts  86.5 us (13%)
  matrix products  37.6 us (6%)
  between operations  25.2 us (4%)
    psum x1, blocking collectives, panels_convert(): return psum(known, net_axis)  126 us
    psum x1, waiting for transfers between devices, panels_convert(): return psum(known, net_axis)  99.3 us
    unnamed x8, other arithmetic  74.8 us
    unnamed x101, local copies, waits for them, and re-layouts  39.1 us
    psum x1, blocking collectives, panels_convert(): known = psum(z_in, mesh_ax)  24.9 us
    all_to_all x1, starting transfers between devices, per_axis_filter(): lax.all_to_all(signal.reshape(3, 1, segment), 'rows', split_axis=2, conca...  21.1 us
    ppermute x6, starting transfers between devices, from_behind(): return lax.ppermute(array, axis, pairs)  16.4 us
    all_to_all x1, starting transfers between devices, per_axis_filter(): lax.all_to_all(signals[0].reshape(signal_count, rows_count, 1, piece_len)...  14.5 us
  transfers between devices with their start and end apart: 22, of which 16 were waited for; matrix products, arithmetic and copies ran while one was open for 22% of the time, Pallas kernels for 0%

profile of v1, /device:TPU:1, one launch (start us, length us, event | category | flops | bytes accessed | tf_op | source)
XLA Modules:
  0.0 660.2 jit_solution(5185480509039228165)
XLA Ops:
  9.9 4.5 collective-permute-start
  15.6 1.4 reduce.3
  18.7 1.4 fusion.349
  22.4 10.8 %gather_fusion = f32[4096,2]{1,0:T(8,128)S(1)} fusion(f32[2,1024]{0,1:T(8,128)S(1)} %copy.178, s32[4096]{0:T(1024)S(1)} %broadcast_clamp_fusion), kind=kCustom, calls=%fused_computation | custom fusion | bytes 81920 | tf_op jit(solution)/shard_map/jit(_take)/gather | solution.py:116
  46.6 1.3 fusion.2
  49.1 1.9 collective-permute-start.1
  53.5 4.1 collective-permute-start.2
  62.5 1.9 collective-permute-start.3
  65.6 3.1 collective-permute-done.3
  71.4 2.1 collective-permute-start.4
  74.4 2.6 collective-permute-done.4
  78.8 1.9 collective-permute-start.5
  81.9 2.5 collective-permute-done.5
  85.7 3.7 copy.151
  90.0 20.4 %reduce.4 = f32[4096,3]{1,0:T(8,128)} reduce(f32[4096,1,3]{2,1,0:T(1,128)} %bitcast.335, f32[]{:T(128)} %broadcast.734), dimensions={1}, to_apply=%bitcast.265.reduce_sub_computation | reduce | bytes 98308
  110.4 3.7 reshape.486
  114.1 21.1 %all-to-all-start = ((f32[8,1,1536]{2,1,0:T(1,128)}), f32[8,1,1536]{2,1,0:T(1,128)S(1)}, u32[]{:S(2)}, u32[]{:S(2)}) async-start(f32[8,1,1536]{2,1,0:T(1,128)} %reshape.486), calls=%async_computation | async-start | bytes 98304 | tf_op jit(solution)/shard_map/all_to_all | solution.py:144
  135.2 2.2 convolution_bitcast_fusion.16
  137.4 4.8 all-to-all-done
  143.0 4.4 reshape.487
  147.4 2.2 copy.231
  150.8 2.0 copy.153
  152.8 4.3 reduce.6
  157.0 2.5 reshape.488
  159.5 14.5 %all-to-all-start.1 = ((f32[32,1,384]{2,1,0:T(1,128)}), f32[32,1,384]{2,1,0:T(1,128)S(1)}, u32[]{:S(2)}, u32[]{:S(2)}) async-start(f32[32,1,384]{2,1,0:T(1,128)} %reshape.488), calls=%async_computation.1 | async-start | bytes 98304 | tf_op jit(solution)/shard_map/all_to_all | solution.py:152
  175.7 3.3 reduce.8
  181.3 6.9 %all-to-all-start.2 = ((f32[32,1,384]{2,1,0:T(1,128)}), f32[32,1,384]{2,1,0:T(1,128)S(1)}, u32[]{:S(2)}, u32[]{:S(2)}) async-start(f32[32,1,384]{2,1,0:T(1,128)} %reshape.490), calls=%async_computation.2 | async-start | bytes 98304 | tf_op jit(solution)/shard_map/all_to_all | solution.py:159
  192.8 2.5 all-to-all-done.2
  199.2 2.3 multiply_add_fusion.1
  203.5 4.9 all-to-all-start.3
  208.4 1.4 pad_maximum_fusion.4
  210.8 4.8 all-to-all-done.3
  215.7 3.9 all-to-all-start.5
  222.9 4.1 all-to-all-done.5
  227.0 3.4 all-to-all-start.4
  233.1 4.3 all-to-all-done.4
  237.4 3.5 all-to-all-start.6
  241.8 6.3 all-to-all-done.6
  254.1 2.4 copy.188
  256.5 19.4 %reduce.12 = f32[4096,3]{1,0:T(8,128)} reduce(f32[4096,1,3]{2,1,0:T(1,128)S(1)} %bitcast.337, f32[]{:T(128)} %broadcast.734), dimensions={1}, to_apply=%bitcast.275.reduce_sub_computation | reduce | bytes 98308
  276.0 3.7 reshape.496
  279.7 3.6 all-to-all-start.7
  283.3 2.4 copy.193
  285.8 19.4 %reduce.16 = f32[4096,3]{1,0:T(8,128)} reduce(f32[4096,1,3]{2,1,0:T(1,128)S(1)} %bitcast.338, f32[]{:T(128)} %broadcast.734), dimensions={1}, to_apply=%bitcast.279.reduce_sub_computation | reduce | bytes 98308
  305.2 3.7 reshape.500
  309.0 6.9 %all-to-all-start.9 = ((f32[8,1,1536]{2,1,0:T(1,128)}), f32[8,1,1536]{2,1,0:T(1,128)S(1)}, u32[]{:S(2)}, u32[]{:S(2)}) async-start(f32[8,1,1536]{2,1,0:T(1,128)} %reshape.500), calls=%async_computation.9 | async-start | bytes 98304 | tf_op jit(solution)/shard_map/all_to_all | solution.py:209
  317.6 3.0 reshape.497
  320.6 4.0 copy.190
  324.6 3.3 reduce.14
  329.1 6.8 %all-to-all-start.8 = ((f32[32,1,384]{2,1,0:T(1,128)}), f32[32,1,384]{2,1,0:T(1,128)S(1)}, u32[]{:S(2)}, u32[]{:S(2)}) async-start(f32[32,1,384]{2,1,0:T(1,128)} %reshape.498), calls=%async_computation.8 | async-start | bytes 98304 | tf_op jit(solution)/shard_map/all_to_all | solution.py:218
  336.0 24.9 %all-reduce.2 = (f32[3,64,64]{2,1,0:T(8,128)S(1)}, f32[64,3]{0,1:T(4,128)S(1)}) all-reduce(f32[3,64,64]{2,1,0:T(8,128)S(1)} %pad_maximum_fusion.6, f32[64,3]{0,1:T(4,128)S(1)} %fusion.359), channel_id=1, replica_groups=mesh['rows'=8,'cols'=32] {'rows'}, use_global_device_ids=true, to_apply=%region_4.0 | all-reduce | flops 12480 | bytes 99840 | tf_op jit(solution)/shard_map/psum | solution.py:12
  360.8 125.9 %all-reduce = (f32[3,64,64]{2,1,0:T(8,128)S(1)}, f32[64,3]{0,1:T(4,128)S(1)}) all-reduce(f32[3,64,64]{2,1,0:T(8,128)S(1)} %get-tuple-element.9, f32[64,3]{0,1:T(4,128)S(1)} %get-tuple-element.10), channel_id=1, replica_groups=mesh['rows'=8,'cols'=32] {'cols'}, use_global_device_ids=true, to_apply=%region_5.0 | all-reduce | flops 12480 | bytes 99840 | tf_op jit(solution)/shard_map/psum | solution.py:13
  487.5 3.0 reshape.501
  490.5 4.0 copy.195
  494.5 3.3 reduce.18
  499.1 9.4 %all-to-all-start.10 = ((f32[32,1,384]{2,1,0:T(1,128)}), f32[32,1,384]{2,1,0:T(1,128)S(1)}, u32[]{:S(2)}, u32[]{:S(2)}) async-start(f32[32,1,384]{2,1,0:T(1,128)} %reshape.502), calls=%async_computation.10 | async-start | bytes 98304 | tf_op jit(solution)/shard_map/all_to_all | solution.py:225
  513.2 2.6 all-to-all-done.10
  521.5 4.9 all-to-all-start.12
  528.0 5.6 all-to-all-done.12
  533.7 3.9 all-to-all-start.11
  539.6 5.4 all-to-all-done.11
  547.4 4.2 all-to-all-start.13
  551.6 99.3 %all-reduce.7.cloned.1.call-done = (f32[3,128,64]{1,2,0:T(8,128)}, f32[3,128,64]{1,2,0:T(8,128)}) async-done(((f32[3,128,64]{1,2,0:T(8,128)}, f32[3,128,64]{1,2,0:T(8,128)}), (f32[3,128,64]{1,2,0:T(8,128)}, f32[3,128,64]{1,2,0:T(8,128)})) %all-reduce.7.cloned.1.call-update) | async-done | bytes 196624 | tf_op jit(solution)/shard_map/psum | solution.py:13
  650.9 1.6 broadcast_multiply_fusion.1
  (239 shorter events, 81.4 us)
Async XLA Ops:
  8.0 12.8 %copy-start.25 = (f32[64]{0:T(128)}, f32[64]{0:T(128)S(1)}, u32[]{:S(2)}) copy-start(f32[64]{0:T(128)S(1)} %get-tuple-element.32) | copy-start | bytes 772
  8.0 12.8 %copy-start.28 = (f32[64]{0:T(128)}, f32[64]{0:T(128)S(1)}, u32[]{:S(2)}) copy-start(f32[64]{0:T(128)S(1)} %get-tuple-element.33) | copy-start | bytes 772
  8.0 12.8 %copy-start.31 = (f32[64]{0:T(128)}, f32[64]{0:T(128)S(1)}, u32[]{:S(2)}) copy-start(f32[64]{0:T(128)S(1)} %get-tuple-element.34) | copy-start | bytes 772
  9.2 37.3 %copy-start = (bf16[64,4096]{1,0:T(8,128)(2,1)}, bf16[64,4096]{1,0:T(8,128)(2,1)S(1)}, u32[]{:S(2)}) copy-start(bf16[64,4096]{1,0:T(8,128)(2,1)S(1)} %fusion.33) | copy-start | bytes 1572868
  9.3 24.7 %copy-start.12 = (bf16[3,128,64]{1,2,0:T(8,128)(2,1)S(1)}, bf16[3,128,64]{1,2,0:T(8,128)(2,1)}, u32[]{:S(2)}) copy-start(bf16[3,128,64]{1,2,0:T(8,128)(2,1)} %param.12) | copy-start | bytes 147460
  9.9 36.6 %collective-permute-start = (bf16[64,256]{1,0:T(8,128)(2,1)}, bf16[64,256]{1,0:T(8,128)(2,1)}, u32[]{:S(2)}, u32[]{:S(2)}) collective-permute-start(bf16[64,256]{1,0:T(8,128)(2,1)} %slice.140), channel_id=1, source_target_pairs={{0,1},{1,2},{2,3},{3,4},{4,5},{5,6},{6,7},{7,8},{8,9},{9,10},{10,1... | collective-permute-start | bytes 98312 | tf_op jit(solution)/shard_map/ppermute | solution.py:19
  21.5 12.4 %copy-start.26 = (f32[64]{0:T(128)S(1)}, f32[64]{0:T(128)}, u32[]{:S(2)}) copy-start(f32[64]{0:T(128)} %copy-done.25) | copy-start | bytes 772
  21.5 12.5 %copy-start.29 = (f32[64]{0:T(128)S(1)}, f32[64]{0:T(128)}, u32[]{:S(2)}) copy-start(f32[64]{0:T(128)} %copy-done.28) | copy-start | bytes 772
  21.5 12.5 %copy-start.32 = (f32[64]{0:T(128)S(1)}, f32[64]{0:T(128)}, u32[]{:S(2)}) copy-start(f32[64]{0:T(128)} %copy-done.31) | copy-start | bytes 772
  33.2 1.3 copy-start.24
  33.2 1.3 copy-start.37
  33.2 2.3 copy-start.17
  33.3 13.3 %copy-start.11 = (bf16[3,128,64]{1,2,0:T(8,128)(2,1)S(1)}, bf16[3,128,64]{1,2,0:T(8,128)(2,1)}, u32[]{:S(2)}) copy-start(bf16[3,128,64]{1,2,0:T(8,128)(2,1)} %param.13) | copy-start | bytes 147460
  35.5 12.3 %copy-start.6 = (f32[2,64,64]{2,1,0:T(8,128)}, f32[2,64,64]{2,1,0:T(8,128)S(1)}, u32[]{:S(2)}) copy-start(f32[2,64,64]{2,1,0:T(8,128)S(1)} %select_bitcast_fusion) | copy-start | bytes 98308
  47.9 0.8 copy-start.21
  47.9 0.8 copy-start.27
  47.9 0.8 copy-start.30
  47.9 0.8 copy-start.33
  49.1 3.1 collective-permute-start.1
  53.5 5.1 collective-permute-start.2
  58.0 1.1 copy-start.8
  62.5 6.2 collective-permute-start.3
  71.4 5.6 collective-permute-start.4
  78.4 5.9 copy-start.4
  78.5 56.7 %copy-start.2 = (bf16[64,4096]{1,0:T(8,128)(2,1)}, bf16[64,4096]{1,0:T(8,128)(2,1)S(1)}, u32[]{:S(2)}) copy-start(bf16[64,4096]{1,0:T(8,128)(2,1)S(1)} %get-tuple-element.13) | copy-start | bytes 1572868
  78.8 5.6 collective-permute-start.5
  81.9 3.2 copy-start.34
  114.1 28.1 %all-to-all-start = ((f32[8,1,1536]{2,1,0:T(1,128)}), f32[8,1,1536]{2,1,0:T(1,128)S(1)}, u32[]{:S(2)}, u32[]{:S(2)}) async-start(f32[8,1,1536]{2,1,0:T(1,128)} %reshape.486), calls=%async_computation | async-start | bytes 98304 | tf_op jit(solution)/shard_map/all_to_all | solution.py:144
  143.0 6.9 %copy-start.35 = (f32[8]{0:T(128)S(1)}, f32[8]{0:T(128)}, u32[]{:S(2)}) copy-start(f32[8]{0:T(128)} %get-tuple-element.42) | copy-start | bytes 100
  143.0 6.9 %copy-start.36 = (f32[8]{0:T(128)S(1)}, f32[8]{0:T(128)}, u32[]{:S(2)}) copy-start(f32[8]{0:T(128)} %get-tuple-element.43) | copy-start | bytes 100
  157.0 17.9 %copy-start.13 = (f32[3,8,1,512]{3,1,0,2:T(8,128)S(1)}, f32[3,8,1,512]{3,1,0,2:T(8,128)}, u32[]{:S(2)}) copy-start(f32[3,8,1,512]{3,1,0,2:T(8,128)} %get-tuple-element.25) | copy-start | bytes 147460
  159.5 21.8 %all-to-all-start.1 = ((f32[32,1,384]{2,1,0:T(1,128)}), f32[32,1,384]{2,1,0:T(1,128)S(1)}, u32[]{:S(2)}, u32[]{:S(2)}) async-start(f32[32,1,384]{2,1,0:T(1,128)} %reshape.488), calls=%async_computation.1 | async-start | bytes 98304 | tf_op jit(solution)/shard_map/all_to_all | solution.py:152
  181.3 14.1 %all-to-all-start.2 = ((f32[32,1,384]{2,1,0:T(1,128)}), f32[32,1,384]{2,1,0:T(1,128)S(1)}, u32[]{:S(2)}, u32[]{:S(2)}) async-start(f32[32,1,384]{2,1,0:T(1,128)} %reshape.490), calls=%async_computation.2 | async-start | bytes 98304 | tf_op jit(solution)/shard_map/all_to_all | solution.py:159
  198.4 21.2 %copy-start.1 = (bf16[64,4096]{1,0:T(8,128)(2,1)S(1)}, bf16[64,4096]{1,0:T(8,128)(2,1)}, u32[]{:S(2)}) copy-start(bf16[64,4096]{1,0:T(8,128)(2,1)} %copy-done) | copy-start | bytes 1572868
  198.4 21.2 %copy-start.3 = (bf16[64,4096]{1,0:T(8,128)(2,1)S(1)}, bf16[64,4096]{1,0:T(8,128)(2,1)}, u32[]{:S(2)}) copy-start(bf16[64,4096]{1,0:T(8,128)(2,1)} %copy-done.2) | copy-start | bytes 1572868
  198.4 21.2 %copy-start.5 = (bf16[64,4096]{1,0:T(8,128)(2,1)S(1)}, bf16[64,4096]{1,0:T(8,128)(2,1)}, u32[]{:S(2)}) copy-start(bf16[64,4096]{1,0:T(8,128)(2,1)} %copy-done.4) | copy-start | bytes 1572868
  203.5 12.2 %all-to-all-start.3 = ((f32[32,1,384]{2,1,0:T(1,128)}), f32[32,1,384]{2,1,0:T(1,128)S(1)}, u32[]{:S(2)}, u32[]{:S(2)}) async-start(f32[32,1,384]{2,1,0:T(1,128)} %reshape.492), calls=%async_computation.3 | async-start | bytes 98304 | tf_op jit(solution)/shard_map/all_to_all | solution.py:176
  215.7 11.3 %all-to-all-start.5 = ((f32[32,1,384]{2,1,0:T(1,128)}), f32[32,1,384]{2,1,0:T(1,128)S(1)}, u32[]{:S(2)}, u32[]{:S(2)}) async-start(f32[32,1,384]{2,1,0:T(1,128)} %reshape.494), calls=%async_computation.5 | async-start | bytes 98304 | tf_op jit(solution)/shard_map/all_to_all | solution.py:177
  219.6 10.8 %copy-start.19 = (f32[1,128,64]{1,2,0:T(8,128)S(1)}, f32[1,128,64]{1,2,0:T(8,128)}, u32[]{:S(2)}) copy-start(f32[1,128,64]{1,2,0:T(8,128)} %convolution_bitcast_fusion.11) | copy-start | bytes 98308
  219.6 10.8 %copy-start.20 = (f32[1,128,64]{1,2,0:T(8,128)S(1)}, f32[1,128,64]{1,2,0:T(8,128)}, u32[]{:S(2)}) copy-start(f32[1,128,64]{1,2,0:T(8,128)} %convolution_bitcast_fusion.12) | copy-start | bytes 98308
  227.0 10.4 %all-to-all-start.4 = ((f32[3,8,512]{2,0,1:T(4,128)}), f32[3,8,512]{2,0,1:T(4,128)S(1)}, u32[]{:S(2)}, u32[]{:S(2)}) async-start(f32[3,8,512]{2,0,1:T(4,128)} %reshape.475), calls=%async_computation.4 | async-start | bytes 131072 | tf_op jit(solution)/shard_map/all_to_all | solution.py:180
  230.3 307.9 %all-reduce.9.cloned.1.call-start = ((), (), s32[]{:S(2)}) async-start(), calls=%async_computation.15 | async-start | bytes 393216 | tf_op jit(solution)/shard_map/psum | solution.py:12
  231.1 18.7 %copy-start.7 = (f32[2,64,64]{2,1,0:T(8,128)S(1)}, f32[2,64,64]{2,1,0:T(8,128)}, u32[]{:S(2)}) copy-start(f32[2,64,64]{2,1,0:T(8,128)} %copy-done.6) | copy-start | bytes 98308
  231.1 18.7 %copy-start.9 = (f32[1,64,64]{2,1,0:T(8,128)S(1)}, f32[1,64,64]{2,1,0:T(8,128)}, u32[]{:S(2)}) copy-start(f32[1,64,64]{2,1,0:T(8,128)} %slice.152) | copy-start | bytes 49156
  237.4 10.7 %all-to-all-start.6 = ((f32[3,8,512]{2,0,1:T(4,128)}), f32[3,8,512]{2,0,1:T(4,128)S(1)}, u32[]{:S(2)}, u32[]{:S(2)}) async-start(f32[3,8,512]{2,0,1:T(4,128)} %reshape.476), calls=%async_computation.6 | async-start | bytes 131072 | tf_op jit(solution)/shard_map/all_to_all | solution.py:187
  249.8 4.3 copy-start.16
  276.0 7.3 %copy-start.14 = (f32[1,64,64]{2,1,0:T(8,128)S(1)}, f32[1,64,64]{2,1,0:T(8,128)}, u32[]{:S(2)}) copy-start(f32[1,64,64]{2,1,0:T(8,128)} %convolution_bitcast_fusion.18) | copy-start | bytes 49156
  276.0 7.3 %copy-start.15 = (f32[1,64,64]{2,1,0:T(8,128)S(1)}, f32[1,64,64]{2,1,0:T(8,128)}, u32[]{:S(2)}) copy-start(f32[1,64,64]{2,1,0:T(8,128)} %convolution_bitcast_fusion.19) | copy-start | bytes 49156
  276.0 7.3 %copy-start.18 = (f32[1,64,64]{2,1,0:T(8,128)S(1)}, f32[1,64,64]{2,1,0:T(8,128)}, u32[]{:S(2)}) copy-start(f32[1,64,64]{2,1,0:T(8,128)} %convolution_bitcast_fusion.17) | copy-start | bytes 49156
  279.7 29.2 %all-to-all-start.7 = ((f32[8,1,1536]{2,1,0:T(1,128)}), f32[8,1,1536]{2,1,0:T(1,128)S(1)}, u32[]{:S(2)}, u32[]{:S(2)}) async-start(f32[8,1,1536]{2,1,0:T(1,128)} %reshape.496), calls=%async_computation.7 | async-start | bytes 98304 | tf_op jit(solution)/shard_map/all_to_all | solution.py:202
  305.2 10.6 %copy-start.10 = (f32[3,4096]{1,0:T(4,128)S(1)}, f32[3,4096]{1,0:T(4,128)}, u32[]{:S(2)}) copy-start(f32[3,4096]{1,0:T(4,128)} %param.9) | copy-start | bytes 147460
  309.0 20.2 %all-to-all-start.9 = ((f32[8,1,1536]{2,1,0:T(1,128)}), f32[8,1,1536]{2,1,0:T(1,128)S(1)}, u32[]{:S(2)}, u32[]{:S(2)}) async-start(f32[8,1,1536]{2,1,0:T(1,128)} %reshape.500), calls=%async_computation.9 | async-start | bytes 98304 | tf_op jit(solution)/shard_map/all_to_all | solution.py:209
  329.1 169.9 %all-to-all-start.8 = ((f32[32,1,384]{2,1,0:T(1,128)}), f32[32,1,384]{2,1,0:T(1,128)S(1)}, u32[]{:S(2)}, u32[]{:S(2)}) async-start(f32[32,1,384]{2,1,0:T(1,128)} %reshape.498), calls=%async_computation.8 | async-start | bytes 98304 | tf_op jit(solution)/shard_map/all_to_all | solution.py:218
  499.1 16.7 %all-to-all-start.10 = ((f32[32,1,384]{2,1,0:T(1,128)}), f32[32,1,384]{2,1,0:T(1,128)S(1)}, u32[]{:S(2)}, u32[]{:S(2)}) async-start(f32[32,1,384]{2,1,0:T(1,128)} %reshape.502), calls=%async_computation.10 | async-start | bytes 98304 | tf_op jit(solution)/shard_map/all_to_all | solution.py:225
  511.6 8.1 %copy-start.22 = (f32[8,32]{1,0:T(8,128)S(1)}, f32[8,32]{1,0:T(8,128)}, u32[]{:S(2)}) copy-start(f32[8,32]{1,0:T(8,128)} %get-tuple-element.40) | copy-start | bytes 3076
  511.6 8.1 %copy-start.23 = (f32[8,32]{1,0:T(8,128)S(1)}, f32[8,32]{1,0:T(8,128)}, u32[]{:S(2)}) copy-start(f32[8,32]{1,0:T(8,128)} %get-tuple-element.41) | copy-start | bytes 3076
  521.5 12.2 %all-to-all-start.12 = ((f32[32,1,384]{2,1,0:T(1,128)}), f32[32,1,384]{2,1,0:T(1,128)S(1)}, u32[]{:S(2)}, u32[]{:S(2)}) async-start(f32[32,1,384]{2,1,0:T(1,128)} %reshape.506), calls=%async_computation.12 | async-start | bytes 98304 | tf_op jit(solution)/shard_map/all_to_all | solution.py:239
  533.7 11.3 %all-to-all-start.11 = ((f32[32,1,384]{2,1,0:T(1,128)}), f32[32,1,384]{2,1,0:T(1,128)S(1)}, u32[]{:S(2)}, u32[]{:S(2)}) async-start(f32[32,1,384]{2,1,0:T(1,128)} %reshape.504), calls=%async_computation.11 | async-start | bytes 98304 | tf_op jit(solution)/shard_map/all_to_all | solution.py:238
  537.6 113.3 %all-reduce.7.cloned.1.call-start = ((), (), s32[]{:S(2)}) async-start(), calls=%async_computation.14 | async-start | bytes 393216 | tf_op jit(solution)/shard_map/psum | solution.py:13
  547.4 105.1 %all-to-all-start.13 = ((f32[3,8,512]{2,0,1:T(4,128)}), f32[3,8,512]{2,0,1:T(4,128)S(1)}, u32[]{:S(2)}, u32[]{:S(2)}) async-start(f32[3,8,512]{2,0,1:T(4,128)} %copy.204), calls=%async_computation.13 | async-start | bytes 131072 | tf_op jit(solution)/shard_map/all_to_all | solution.py:247
Sparse Core Ops, SparseCore 0:
  234.1 65.3 all-reduce.8
  541.8 109.0 all-reduce.6
